TPU v7x, 256 devices: a whole 4x4x8 slice. The times are simulated.
256 devices in a mesh: gx: 4 (over y), gy: 16 (over z, core), gz: 4 (over x).
Axes of the slice: x: 4, y: 4, z: 8, core: 2. Of those that a mesh axis runs over, the one named last changes fastest.
Arguments:
- flux_jacobian_factor: bfloat16 [4, 64, 8, 320, 320], P('gx', 'gy', 'gz'), may hold values from -6 to 6
- mass_over_timestep: float32 [4, 64, 8, 320], P('gx', 'gy', 'gz'), may hold values from 0.5 to 2
- face_jacobian: float32 [4, 64, 8, 3, 80, 160], P('gx', 'gy', 'gz'), may hold values from -1 to 1
- face_flags: int32 [4, 64, 8, 6], P('gx', 'gy', 'gz'), may hold values from 0 to 1, as said below
- right_side: float32 [4, 64, 8, 320], P('gx', 'gy', 'gz'), may hold values from -36 to 36
Outputs:
- update: float32 [4, 64, 8, 320], P('gx', 'gy', 'gz')
Inputs may be any that keep to these rules, and one draw needn't show every extreme that they name: face_flags[e, 2 d] and face_flags[e, 2 d + 1] mark the lower and upper face of element e along dimension d as a wall (1) or open (0); the upper flag of an element along a dimension equals the lower flag of the element after it along that dimension.
All inputs are finite; a program needn't handle non-finite values.
Results may differ from a plain program's by a relative error of at most 0.0003.
Values sent between devices are 32-bit elements; how exact they have to be, the bound alone decides.
No kernel may reach another device: no remote copies, remote signals or barrier semaphores. Data moves between devices by JAX's collectives and lax.ppermute only.
A program may use at most 128 MiB of HBM per device.

v0:
```python
import jax
import jax.numpy as jnp
from jax import lax
from jax.sharding import PartitionSpec as P

VARS = 5
ORDER = 4
KRYLOV = 3
ELEMENT_UNKNOWNS = 320
FACE_UNKNOWNS = 80
full_precision = lax.Precision.HIGHEST
wall_weight = 0.5


def passed_along(block, axis, distance):
    devices = range(lax.axis_size(axis))
    route = [(i - distance, i) for i in devices if i - distance in devices]
    return lax.ppermute(block, axis, route)


def padded_2(cells, sides, width):
    for axis, dim in sides:
        count = lax.axis_size(axis)
        ends = count - 1
        head = lax.slice_in_dim(cells, 0, width, axis=dim)
        tail = lax.slice_in_dim(cells, cells.shape[dim] - width, cells.shape[dim], axis=dim)
        cells = jnp.concatenate(
            [
                lax.ppermute(tail, axis, [(i, (i + 1) % count) for i in range(ends)]),
                cells,
                lax.ppermute(head, axis, [((i + 1) % count, i) for i in range(ends)]),
            ],
            axis=dim,
        )
    return cells


def take_face(field, d, index):
    lead = field.shape[:3]
    cube = field.reshape(lead + (VARS, ORDER, ORDER, ORDER))
    face = lax.index_in_dim(cube, index, axis=4 + d, keepdims=False)
    return face.reshape(lead + (FACE_UNKNOWNS,))


def put_face(values, d, index):
    lead = values.shape[:3]
    cube = jnp.zeros(lead + (VARS, ORDER, ORDER, ORDER), values.dtype)
    spot = (slice(None),) * (4 + d) + (index,)
    cube = cube.at[spot].set(values.reshape(lead + (VARS, ORDER, ORDER)))
    return cube.reshape(lead + (ELEMENT_UNKNOWNS,))


def face_flux(matrix, left_trace, right_trace):
    paired = jnp.concatenate([left_trace, right_trace], axis=-1)
    return jnp.einsum("abcfg,abcg->abcf", matrix, paired, precision=full_precision)


def couple_faces(field, d, w_dim, face_flags, below_trace, top_flux):
    count = field.shape[d]
    lower_trace = take_face(field, d, 0)
    upper_trace = take_face(field, d, ORDER - 1)
    lower_flux = face_flux(w_dim, below_trace, lower_trace)
    upper_flux = jnp.concatenate(
        [lax.slice_in_dim(lower_flux, 1, count, axis=d), top_flux(lower_flux, upper_trace)], axis=d
    )
    lower_open = (1 - face_flags[..., 2 * d : 2 * d + 1]).astype(jnp.float32)
    upper_open = (1 - face_flags[..., 2 * d + 1 : 2 * d + 2]).astype(jnp.float32)
    lower_part = -lower_open * lower_flux + (1.0 - lower_open) * wall_weight * lower_trace
    upper_part = upper_open * upper_flux + (1.0 - upper_open) * wall_weight * upper_trace
    return put_face(lower_part, d, 0) + put_face(upper_part, d, ORDER - 1)


def neighbour(padded, d, start, length):
    spots = []
    for axis_pos in range(3):
        if axis_pos == d:
            spots.append(slice(start, start + length))
        else:
            spots.append(slice(1, padded.shape[axis_pos] - 1))
    return padded[tuple(spots)]


def ghost_faces(field, padded, d, w_dim, w_top, face_flags):
    count = field.shape[d]
    below_trace = take_face(neighbour(padded, d, 0, count), d, ORDER - 1)
    above_top = take_face(neighbour(padded, d, count + 1, 1), d, 0)

    def top_flux(lower_flux, upper_trace):
        return face_flux(w_top, lax.slice_in_dim(upper_trace, count - 1, count, axis=d), above_top)

    return couple_faces(field, d, w_dim, face_flags, below_trace, top_flux)


def least_squares(columns, start_norm):
    count = len(columns)
    cosines = []
    sine_terms = []
    target_values = [start_norm] + [jnp.zeros((), jnp.float32) for i in range(count)]
    triangle = []
    for j in range(count):
        column = list(columns[j])
        for i in range(j):
            first_entry = column[i]
            second_entry = column[i + 1]
            column[i] = cosines[i] * first_entry + sine_terms[i] * second_entry
            column[i + 1] = -sine_terms[i] * first_entry + cosines[i] * second_entry
        radius = jnp.sqrt(column[j] * column[j] + column[j + 1] * column[j + 1])
        cosine = column[j] / radius
        sine_part = column[j + 1] / radius
        cosines.append(cosine)
        sine_terms.append(sine_part)
        column[j] = radius
        target_values[j + 1] = -sine_part * target_values[j]
        target_values[j] = cosine * target_values[j]
        triangle.append(column[: j + 1])
    weights = [None] * count
    for i in reversed(range(count)):
        running = target_values[i]
        for k in range(i + 1, count):
            running = running - triangle[k][i] * weights[k]
        weights[i] = running / triangle[i][i]
    return weights


def precond_apply(precond, vector):
    return jnp.einsum("abcij,abcj->abci", precond, vector, precision=full_precision)


def shards(flux_jacobian_factor, mass_over_timestep, face_jacobian, face_flags, right_side):
    gram_part = jnp.einsum(
        "abcki,abckj->abcij",
        flux_jacobian_factor,
        flux_jacobian_factor,
        preferred_element_type=jnp.float32,
    )
    identity = jnp.eye(ELEMENT_UNKNOWNS, dtype=jnp.float32)
    jacobian = gram_part / ELEMENT_UNKNOWNS + mass_over_timestep[..., None] * identity
    factor_lower = jnp.linalg.cholesky(jacobian)
    lower_inverse = jax.scipy.linalg.solve_triangular(
        factor_lower, jnp.broadcast_to(identity, jacobian.shape), lower=True
    )
    precond = jnp.einsum(
        "abcki,abckj->abcij", lower_inverse, lower_inverse, precision=full_precision
    )
    top_blocks = (
        passed_along(face_jacobian[0:1, :, :, 0], "gx", -1),
        passed_along(face_jacobian[:, 0:1, :, 1], "gy", -1),
        passed_along(face_jacobian[:, :, 0:1, 2], "gz", -1),
    )
    start_norm = jnp.sqrt(lax.psum(jnp.sum(right_side * right_side), ("gx", "gy", "gz")))
    krylov_basis = [right_side / start_norm]
    columns = []
    for j in range(KRYLOV):
        direction = precond_apply(precond, krylov_basis[j])
        mapped = jnp.einsum("abcij,abcj->abci", jacobian, direction, precision=full_precision)
        padded = padded_2(direction, (("gx", 0), ("gy", 1), ("gz", 2)), 1)
        for d in range(3):
            mapped = mapped + ghost_faces(
                direction, padded, d, face_jacobian[:, :, :, d], top_blocks[d], face_flags
            )
        local_dots = jnp.stack([jnp.sum(vector * mapped) for vector in krylov_basis])
        project = lax.psum(local_dots, ("gx", "gy", "gz"))
        for i in range(len(krylov_basis)):
            mapped = mapped - project[i] * krylov_basis[i]
        length = jnp.sqrt(lax.psum(jnp.sum(mapped * mapped), ("gx", "gy", "gz")))
        columns.append([project[i] for i in range(len(krylov_basis))] + [length])
        if j + 1 < KRYLOV:
            krylov_basis.append(mapped / length)
    weights = least_squares(columns, start_norm)
    combined = weights[0] * krylov_basis[0]
    for j in range(1, KRYLOV):
        combined = combined + weights[j] * krylov_basis[j]
    return precond_apply(precond, combined)


def solution(mesh):
    in_specs = (
        P("gx", "gy", "gz", None, None),
        P("gx", "gy", "gz", None),
        P("gx", "gy", "gz", None, None, None),
        P("gx", "gy", "gz", None),
        P("gx", "gy", "gz", None),
    )
    out_specs = P("gx", "gy", "gz", None)
    return jax.shard_map(shards, mesh=mesh, in_specs=in_specs, out_specs=out_specs, check_vma=False)
```

profile of v0, /device:TPU:1, one launch (start us, length us, event | category | flops | bytes accessed | tf_op | source)
XLA Modules:
  0.0 1564.7 jit_solution(18332297160623081579)
XLA Ops:
  1.8 4.1 multiply_add_fusion
  6.0 5.4 copy.356
  11.4 3.7 fusion.6
  15.1 1.9 copy-done.4
  17.0 93.8 %custom-call.26 = f32[1,4,2,128,128]{4,3,2,1,0:T(8,128)S(1)} custom-call(f32[1,4,2,128,128]{4,3,2,1,0:T(8,128)S(1)} %cholesky.211), custom_call_target="Cholesky" | custom-call | tf_op jit(solution)/shard_map/jit(cholesky)/cholesky | solution.py:138
  110.9 78.6 %custom-call.27 = f32[1,4,2,1,128,128]{4,5,3,2,1,0:T(8,128)S(1)} custom-call(f32[1,4,2,1,128,128]{5,4,3,2,1,0:T(8,128)S(1)} %select_bitcast_fusion.1), custom_call_target="InvertDiagBlocksLowerTriangular" | custom-call | tf_op jit(solution)/shard_map/jit(cholesky)/cholesky | solution.py:138
  189.5 2.3 cholesky.187
  191.8 3.0 constant_dynamic-update-slice_fusion.2
  194.8 2.3 fusion.15
  197.2 94.0 %custom-call.28 = f32[1,4,2,128,128]{4,3,2,1,0:T(8,128)S(1)} custom-call(f32[1,4,2,128,128]{4,3,2,1,0:T(8,128)S(1)} %cholesky.215), custom_call_target="Cholesky" | custom-call | tf_op jit(solution)/shard_map/jit(cholesky)/cholesky | solution.py:138
  292.2 78.6 %custom-call.29 = f32[1,4,2,1,128,128]{4,5,3,2,1,0:T(8,128)S(1)} custom-call(f32[1,4,2,1,128,128]{5,4,3,2,1,0:T(8,128)S(1)} %get-tuple-element.264), custom_call_target="InvertDiagBlocksLowerTriangular" | custom-call | tf_op jit(solution)/shard_map/jit(cholesky)/cholesky | solution.py:138
  372.1 1.9 fusion.17
  374.0 46.9 %custom-call.30 = f32[1,4,2,64,64]{4,3,2,1,0:T(8,128)S(1)} custom-call(f32[1,4,2,64,64]{4,3,2,1,0:T(8,128)S(1)} %fusion.17), custom_call_target="Cholesky" | custom-call | tf_op jit(solution)/shard_map/jit(cholesky)/cholesky | solution.py:138
  422.5 2.7 bitcast_select_fusion
  425.3 1.8 copy-done.3
  427.1 8.4 while.19
  427.7 3.6 bitcast_dynamic-update-slice_fusion.2
  431.9 3.5 bitcast_dynamic-update-slice_fusion.2
  437.0 236.9 %custom-call.31 = f32[4,2,3,128,128]{3,4,2,1,0:T(8,128)} custom-call(f32[4,2,3,128,128]{4,3,2,1,0:T(8,128)S(1)} %pad_maximum_fusion), custom_call_target="InvertDiagBlocksLowerTriangular" | custom-call | tf_op jit(solution)/shard_map/jit(_solve_triangular)/vmap(vmap())/triangular_solve | solution.py:139
  674.0 2.3 fusion.43
  676.3 2.3 convolution_subtract_fusion
  678.6 2.2 fusion.56
  681.0 3.4 fusion.12
  684.4 3.3 fusion.70
  688.3 10.2 fusion
  698.5 81.4 %psum.49 = f32[]{:T(128)} all-reduce(f32[]{:T(128)} %multiply_reduce_fusion.2), channel_id=1, replica_groups=mesh['gx'=4,'gy'=16,'gz'=4] {'gx','gy','gz'}, use_global_device_ids=true, to_apply=%region_7.8 | all-reduce | flops 1 | bytes 8 | tf_op jit(solution)/shard_map/psum | solution.py:150
  780.5 5.7 fusion.108
  786.2 1.9 collective-permute-start
  792.3 2.8 collective-permute-start.5
  813.4 4.9 fusion.106
  826.2 1.6 reshape_squeeze.144
  857.6 2.7 collective-permute-start.3
  860.4 1.9 collective-permute-start.4
  867.2 4.9 collective-permute-start.6
  896.6 1.7 fusion.148
  900.0 1.8 pad_add_fusion.7
  911.7 78.9 %psum.50 = f32[]{:T(128)} all-reduce(f32[]{:T(128)} %get-tuple-element.260), channel_id=1, replica_groups=mesh['gx'=4,'gy'=16,'gz'=4] {'gx','gy','gz'}, use_global_device_ids=true, to_apply=%region_9.10 | all-reduce | flops 1 | bytes 8 | tf_op jit(solution)/shard_map/psum | solution.py:162
  991.8 72.8 %psum.51 = f32[]{:T(128)} all-reduce(f32[]{:T(128)} %multiply_reduce_fusion.1), channel_id=1, replica_groups=mesh['gx'=4,'gy'=16,'gz'=4] {'gx','gy','gz'}, use_global_device_ids=true, to_apply=%region_11.12 | all-reduce | flops 1 | bytes 8 | tf_op jit(solution)/shard_map/psum | solution.py:165
  1066.0 5.7 fusion.104
  1072.3 3.2 collective-permute-start.9
  1075.5 1.7 collective-permute-start.10
  1080.1 4.9 fusion.102
  1092.5 1.6 reshape_squeeze.161
  1115.7 3.6 collective-permute-start.11
  1119.4 1.9 collective-permute-start.12
  1123.0 1.9 add.377
  1126.3 2.4 collective-permute-start.13
  1142.1 1.7 fusion.146
  1151.5 1.8 pad_add_fusion.4
  1166.2 77.7 %psum.52 = f32[2]{0:T(128)S(1)} all-reduce(f32[2]{0:T(128)S(1)} %pad_maximum_fusion.37), channel_id=1, replica_groups=mesh['gx'=4,'gy'=16,'gz'=4] {'gx','gy','gz'}, use_global_device_ids=true, to_apply=%region_14.15 | all-reduce | flops 2 | bytes 16 | tf_op jit(solution)/shard_map/psum | solution.py:162
  1244.5 1.8 multiply_reduce_fusion
  1246.3 72.7 %psum.53 = f32[]{:T(128)} all-reduce(f32[]{:T(128)} %get-tuple-element.257), channel_id=1, replica_groups=mesh['gx'=4,'gy'=16,'gz'=4] {'gx','gy','gz'}, use_global_device_ids=true, to_apply=%region_16.17 | all-reduce | flops 1 | bytes 8 | tf_op jit(solution)/shard_map/psum | solution.py:165
  1319.7 5.7 fusion.100
  1326.0 3.2 collective-permute-start.15
  1333.6 4.9 fusion.98
  1346.1 1.6 reshape_squeeze.177
  1350.2 1.6 reshape_squeeze.171
  1368.4 4.0 collective-permute-start.17
  1372.4 1.9 collective-permute-start.18
  1396.8 2.0 pad_maximum_fusion.38
  1398.8 78.6 %psum.54 = f32[3]{0:T(128)S(1)} all-reduce(f32[3]{0:T(128)S(1)} %pad_maximum_fusion.38), channel_id=1, replica_groups=mesh['gx'=4,'gy'=16,'gz'=4] {'gx','gy','gz'}, use_global_device_ids=true, to_apply=%region_20.21 | all-reduce | flops 3 | bytes 24 | tf_op jit(solution)/shard_map/psum | solution.py:162
  1481.8 2.5 fusion.110
  1484.3 72.6 %psum.55 = f32[]{:T(128)} all-reduce(f32[]{:T(128)} %fusion.110), channel_id=1, replica_groups=mesh['gx'=4,'gy'=16,'gz'=4] {'gx','gy','gz'}, use_global_device_ids=true, to_apply=%region_22.23 | all-reduce | flops 1 | bytes 8 | tf_op jit(solution)/shard_map/psum | solution.py:165
  1557.9 5.7 fusion.96
  (386 shorter events, 233.0 us)
Async XLA Ops:
  0.0 1.8 copy-start
  0.0 5.9 copy-start.5
  15.1 1.9 copy-start.4
  425.2 1.9 copy-start.3
  427.1 247.0 %copy-start.8 = (f32[128,320]{0,1:T(8,128)S(1)}, f32[128,320]{0,1:T(8,128)}, u32[]{:S(2)}) copy-start(f32[128,320]{0,1:T(8,128)} %get-tuple-element.267) | copy-start | bytes 491524
  435.4 240.8 %copy-start.7 = (f32[128,320]{0,1:T(8,128)S(1)}, f32[128,320]{0,1:T(8,128)}, u32[]{:S(2)}) copy-start(f32[128,320]{0,1:T(8,128)} %get-tuple-element.266) | copy-start | bytes 491524
  674.0 6.8 slice-start
  680.8 6.8 copy-start.6
  698.4 91.0 %copy-start.2 = (f32[1,4,2,3,80,160]{5,4,3,2,1,0:T(8,128)S(1)}, f32[1,4,2,3,80,160]{5,4,3,2,1,0:T(8,128)}, u32[]{:S(2)}) copy-start(f32[1,4,2,3,80,160]{5,4,3,2,1,0:T(8,128)} %param.43) | copy-start | bytes 3686404
  698.5 98.8 %copy-start.12 = (s32[1,4,2,6]{3,2,1,0:T(2,128)S(1)}, s32[1,4,2,6]{3,2,1,0:T(2,128)}, u32[]{:S(2)}) copy-start(s32[1,4,2,6]{3,2,1,0:T(2,128)} %param.44) | copy-start | bytes 580
  786.2 61.6 %collective-permute-start = (f32[1,4,2,320]{3,1,2,0:T(4,128)S(1)}, f32[1,4,2,320]{3,1,2,0:T(4,128)}, u32[]{:S(2)}, u32[]{:S(2)}) collective-permute-start(f32[1,4,2,320]{3,1,2,0:T(4,128)S(1)} %bitcast.397), channel_id=1, source_target_pairs={{0,64},{64,128},{128,192},{1,65},{65,129},{129,193},{2,66},{66,130... | collective-permute-start | bytes 30728 | tf_op jit(solution)/shard_map/ppermute | solution.py:29
  788.1 65.2 %collective-permute-start.1 = (f32[1,4,2,320]{3,1,2,0:T(4,128)S(1)}, f32[1,4,2,320]{3,1,2,0:T(4,128)}, u32[]{:S(2)}, u32[]{:S(2)}) collective-permute-start(f32[1,4,2,320]{3,1,2,0:T(4,128)S(1)} %bitcast.398), channel_id=1, source_target_pairs={{64,0},{128,64},{192,128},{65,1},{129,65},{193,129},{66,2},{130,66... | collective-permute-start | bytes 30728 | tf_op jit(solution)/shard_map/ppermute | solution.py:31
  790.3 117.2 %collective-permute-start.2 = (f32[1,4,2,80,160]{4,3,2,1,0:T(8,128)}, f32[1,4,2,80,160]{4,3,2,1,0:T(8,128)S(1)}, u32[]{:S(2)}, u32[]{:S(2)}) collective-permute-start(f32[1,4,2,80,160]{4,3,2,1,0:T(8,128)} %slice_bitcast_fusion.2), channel_id=1, source_target_pairs={{64,0},{128,64},{192,128},{65,1},{129,65},{193,129},{66,2},{130,66... | collective-permute-start | bytes 1228808 | tf_op jit(solution)/shard_map/ppermute | solution.py:18
  792.3 103.3 %collective-permute-start.5 = (f32[1,1,2,80,160]{4,3,2,1,0:T(8,128)}, f32[1,1,2,80,160]{4,3,2,1,0:T(8,128)S(1)}, u32[]{:S(2)}, u32[]{:S(2)}) collective-permute-start(f32[1,1,2,80,160]{4,3,2,1,0:T(8,128)} %slice_bitcast_fusion.16), channel_id=1, source_target_pairs={{4,0},{8,4},{12,8},{16,12},{20,16},{24,20},{28,24},{32,28},{36,32}... | collective-permute-start | bytes 307208 | tf_op jit(solution)/shard_map/ppermute | solution.py:18
  795.9 107.2 %collective-permute-start.8 = (f32[1,4,1,80,160]{4,3,1,2,0:T(8,128)}, f32[1,4,1,80,160]{4,3,1,2,0:T(8,128)S(1)}, u32[]{:S(2)}, u32[]{:S(2)}) collective-permute-start(f32[1,4,1,80,160]{4,3,1,2,0:T(8,128)} %slice_bitcast_fusion.11), channel_id=1, source_target_pairs={{1,0},{2,1},{3,2},{5,4},{6,5},{7,6},{9,8},{10,9},{11,10},{13,12},{... | collective-permute-start | bytes 614408 | tf_op jit(solution)/shard_map/ppermute | solution.py:18
  842.9 53.6 %copy-start.20 = (f32[4,2]{1,0:T(4,128)}, f32[4,2]{1,0:T(4,128)S(1)}, u32[]{:S(2)}) copy-start(f32[4,2]{1,0:T(4,128)S(1)} %copy.392) | copy-start | bytes 100
  843.7 52.8 %copy-start.21 = (f32[4,2]{1,0:T(4,128)}, f32[4,2]{1,0:T(4,128)S(1)}, u32[]{:S(2)}) copy-start(f32[4,2]{1,0:T(4,128)S(1)} %copy.394) | copy-start | bytes 100
  857.6 7.6 collective-permute-start.3
  860.4 5.4 collective-permute-start.4
  865.2 0.6 copy-start.17
  867.2 11.3 collective-permute-start.6
  875.7 16.5 %collective-permute-start.7 = (f32[3,6,1,320]{3,1,2,0:T(8,128)}, f32[3,6,1,320]{3,1,2,0:T(8,128)}, u32[]{:S(2)}, u32[]{:S(2)}) collective-permute-start(f32[3,6,1,320]{3,1,2,0:T(8,128)} %get-tuple-element.287), channel_id=1, source_target_pairs={{1,0},{2,1},{3,2},{5,4},{6,5},{7,6},{9,8},{10,9},{11,10},{13,12},{... | collective-permute-start | bytes 69128 | tf_op jit(solution)/shard_map/ppermute | solution.py:31
  883.8 12.7 copy-start.24
  898.4 11.4 copy-start.9
  1072.3 28.7 %collective-permute-start.9 = (f32[1,4,2,320]{3,1,2,0:T(4,128)}, f32[1,4,2,320]{3,1,2,0:T(4,128)}, u32[]{:S(2)}, u32[]{:S(2)}) collective-permute-start(f32[1,4,2,320]{3,1,2,0:T(4,128)} %bitcast.312.clone.2), channel_id=1, source_target_pairs={{0,64},{64,128},{128,192},{1,65},{65,129},{129,193},{2,66},{66,130... | collective-permute-start | bytes 30728 | tf_op jit(solution)/shard_map/ppermute | solution.py:29
  1075.5 31.8 %collective-permute-start.10 = (f32[1,4,2,320]{3,1,2,0:T(4,128)}, f32[1,4,2,320]{3,1,2,0:T(4,128)}, u32[]{:S(2)}, u32[]{:S(2)}) collective-permute-start(f32[1,4,2,320]{3,1,2,0:T(4,128)} %bitcast.312.clone.2), channel_id=1, source_target_pairs={{64,0},{128,64},{192,128},{65,1},{129,65},{193,129},{66,2},{130,66... | collective-permute-start | bytes 30728 | tf_op jit(solution)/shard_map/ppermute | solution.py:31
  1080.1 32.0 %copy-start.22 = (f32[4,2]{1,0:T(4,128)S(1)}, f32[4,2]{1,0:T(4,128)}, u32[]{:S(2)}) copy-start(f32[4,2]{1,0:T(4,128)} %copy.377) | copy-start | bytes 100
  1080.1 32.0 %copy-start.23 = (f32[4,2]{1,0:T(4,128)S(1)}, f32[4,2]{1,0:T(4,128)}, u32[]{:S(2)}) copy-start(f32[4,2]{1,0:T(4,128)} %copy.379) | copy-start | bytes 100
  1115.7 9.2 collective-permute-start.11
  1119.3 42.1 %copy-start.18 = (f32[4,2]{1,0:T(4,128)S(1)}, f32[4,2]{1,0:T(4,128)}, u32[]{:S(2)}) copy-start(f32[4,2]{1,0:T(4,128)} %copy.397) | copy-start | bytes 100
  1119.3 42.1 %copy-start.19 = (f32[4,2]{1,0:T(4,128)S(1)}, f32[4,2]{1,0:T(4,128)}, u32[]{:S(2)}) copy-start(f32[4,2]{1,0:T(4,128)} %copy.401) | copy-start | bytes 100
  1119.4 5.5 collective-permute-start.12
  1126.3 9.2 collective-permute-start.13
  1134.0 23.4 %collective-permute-start.14 = (f32[3,6,1,320]{3,1,2,0:T(8,128)}, f32[3,6,1,320]{3,1,2,0:T(8,128)}, u32[]{:S(2)}, u32[]{:S(2)}) collective-permute-start(f32[3,6,1,320]{3,1,2,0:T(8,128)} %get-tuple-element.285), channel_id=1, source_target_pairs={{1,0},{2,1},{3,2},{5,4},{6,5},{7,6},{9,8},{10,9},{11,10},{13,12},{... | collective-permute-start | bytes 69128 | tf_op jit(solution)/shard_map/ppermute | solution.py:31
  1141.4 0.8 copy-start.25
  1150.1 14.0 copy-start.14
  1150.1 14.0 copy-start.16
  1246.3 85.2 %copy-start.10 = (f32[1,4,2,320]{3,2,1,0:T(2,128)}, f32[1,4,2,320]{3,2,1,0:T(2,128)S(1)}, u32[]{:S(2)}) copy-start(f32[1,4,2,320]{3,2,1,0:T(2,128)S(1)} %get-tuple-element.258) | copy-start | bytes 30724
  1326.0 28.9 %collective-permute-start.15 = (f32[1,4,2,320]{3,1,2,0:T(4,128)}, f32[1,4,2,320]{3,1,2,0:T(4,128)}, u32[]{:S(2)}, u32[]{:S(2)}) collective-permute-start(f32[1,4,2,320]{3,1,2,0:T(4,128)} %bitcast.309.clone.2), channel_id=1, source_target_pairs={{0,64},{64,128},{128,192},{1,65},{65,129},{129,193},{2,66},{66,130... | collective-permute-start | bytes 30728 | tf_op jit(solution)/shard_map/ppermute | solution.py:29
  1329.2 32.0 %collective-permute-start.16 = (f32[1,4,2,320]{3,1,2,0:T(4,128)}, f32[1,4,2,320]{3,1,2,0:T(4,128)}, u32[]{:S(2)}, u32[]{:S(2)}) collective-permute-start(f32[1,4,2,320]{3,1,2,0:T(4,128)} %bitcast.309.clone.2), channel_id=1, source_target_pairs={{64,0},{128,64},{192,128},{65,1},{129,65},{193,129},{66,2},{130,66... | collective-permute-start | bytes 30728 | tf_op jit(solution)/shard_map/ppermute | solution.py:31
  1368.4 7.9 collective-permute-start.17
  1372.4 5.3 collective-permute-start.18
  1378.5 4.9 collective-permute-start.19
  1381.9 10.9 collective-permute-start.20
  1384.7 11.4 copy-start.11
  1384.7 11.4 copy-start.13
  1384.7 11.4 copy-start.15
  1391.9 172.3 %copy-start.1 = (bf16[1,4,2,320,320]{4,3,2,1,0:T(8,128)(2,1)S(1)}, bf16[1,4,2,320,320]{4,3,2,1,0:T(8,128)(2,1)}, u32[]{:S(2)}) copy-start(bf16[1,4,2,320,320]{4,3,2,1,0:T(8,128)(2,1)} %param.41) | copy-start | bytes 4915204
where the time goes:
time: 1580 us; the launch traced here: 1560 us
  other arithmetic  709 us (45%)
  blocking collectives  535 us (34%)
  local copies, waits for them, and re-layouts  171 us (11%)
  matrix products  87.4 us (6%)
  starting transfers between devices  47.4 us (3%)
    another operation x14, other arithmetic, shards(): factor_lower = jnp.linalg.cholesky(jacobian)  394 us
    another operation x8, other arithmetic, shards(): jax.scipy.linalg.solve_triangular(factor_lower, jnp.broadcast_to(identity...  241 us
    psum x3, blocking collectives, shards(): project = lax.psum(local_dots, ('gx', 'gy', 'gz'))  235 us
    psum x3, blocking collectives, shards(): length = jnp.sqrt(lax.psum(jnp.sum(mapped * mapped), ('gx', 'gy', 'gz')))  218 us
    psum x1, blocking collectives, shards(): lax.psum(jnp.sum(right_side * right_side), ('gx', 'gy', 'gz'))  81.4 us
    another operation x48, local copies, waits for them, and re-layouts, take_face(): return face.reshape(lead + (FACE_UNKNOWNS,))  43.4 us
  transfers between devices with their start and end apart: 21, of which 1 were waited for; matrix products, arithmetic and copies ran while one was open for 13% of the time, Pallas kernels for 0%

commit v1 on v0

--- a/solution.py
+++ b/solution.py
@@ -159,7 +159,7 @@
                 direction, padded, d, face_jacobian[:, :, :, d], top_blocks[d], face_flags
             )
         local_dots = jnp.stack([jnp.sum(vector * mapped) for vector in krylov_basis])
-        project = lax.psum(local_dots, ("gx", "gy", "gz"))
+        project = lax.psum(lax.psum(local_dots, "gx"), ("gy", "gz"))
         for i in range(len(krylov_basis)):
             mapped = mapped - project[i] * krylov_basis[i]
         length = jnp.sqrt(lax.psum(jnp.sum(mapped * mapped), ("gx", "gy", "gz")))

time: 1580 us -> 1760 us (1.11)
  blocking collectives: 535 us -> 713 us
    psum x3 -> x6, blocking collectives: 235 us -> 400 us  [shards(): project = lax.psum(lax.psum(local_dots, 'gx'), ('gy', 'gz'))]
  transfers between devices with their start and end apart: 21 -> 21, of which waited for: 1 -> 1; matrix products, arithmetic and copies ran while one was open for 13% -> 12% of each run, Pallas kernels for 0% -> 0%
where the time goes in v1:
time: 1760 us; the launch traced here: 1740 us
  blocking collectives  713 us (41%)
  other arithmetic  709 us (40%)
  local copies, waits for them, and re-layouts  171 us (10%)
  matrix products  87.4 us (5%)
  starting transfers between devices  49.1 us (3%)
    psum x6, blocking collectives, shards(): project = lax.psum(lax.psum(local_dots, 'gx'), ('gy', 'gz'))  400 us
    another operation x14, other arithmetic, shards(): factor_lower = jnp.linalg.cholesky(jacobian)  394 us
    another operation x8, other arithmetic, shards(): jax.scipy.linalg.solve_triangular(factor_lower, jnp.broadcast_to(identity...  241 us
    psum x3, blocking collectives, shards(): length = jnp.sqrt(lax.psum(jnp.sum(mapped * mapped), ('gx', 'gy', 'gz')))  231 us
    psum x1, blocking collectives, shards(): lax.psum(jnp.sum(right_side * right_side), ('gx', 'gy', 'gz'))  81.4 us
    another operation x48, local copies, waits for them, and re-layouts, take_face(): return face.reshape(lead + (FACE_UNKNOWNS,))  43.4 us
  transfers between devices with their start and end apart: 21, of which 1 were waited for; matrix products, arithmetic and copies ran while one was open for 12% of the time, Pallas kernels for 0%

profile of v1, /device:TPU:1, one launch (start us, length us, event | category | flops | bytes accessed | tf_op | source)
XLA Modules:
  0.0 1744.3 jit_solution(93404782153074919)
XLA Ops:
  1.8 4.1 multiply_add_fusion
  6.0 5.4 copy.356
  11.4 3.7 fusion.6
  15.1 1.9 copy-done.4
  17.0 93.8 %custom-call.26 = f32[1,4,2,128,128]{4,3,2,1,0:T(8,128)S(1)} custom-call(f32[1,4,2,128,128]{4,3,2,1,0:T(8,128)S(1)} %cholesky.211), custom_call_target="Cholesky" | custom-call | tf_op jit(solution)/shard_map/jit(cholesky)/cholesky | solution.py:138
  110.9 78.6 %custom-call.27 = f32[1,4,2,1,128,128]{4,5,3,2,1,0:T(8,128)S(1)} custom-call(f32[1,4,2,1,128,128]{5,4,3,2,1,0:T(8,128)S(1)} %select_bitcast_fusion.1), custom_call_target="InvertDiagBlocksLowerTriangular" | custom-call | tf_op jit(solution)/shard_map/jit(cholesky)/cholesky | solution.py:138
  189.5 2.3 cholesky.187
  191.8 3.0 constant_dynamic-update-slice_fusion.2
  194.8 2.3 fusion.15
  197.2 94.0 %custom-call.28 = f32[1,4,2,128,128]{4,3,2,1,0:T(8,128)S(1)} custom-call(f32[1,4,2,128,128]{4,3,2,1,0:T(8,128)S(1)} %cholesky.215), custom_call_target="Cholesky" | custom-call | tf_op jit(solution)/shard_map/jit(cholesky)/cholesky | solution.py:138
  292.2 78.6 %custom-call.29 = f32[1,4,2,1,128,128]{4,5,3,2,1,0:T(8,128)S(1)} custom-call(f32[1,4,2,1,128,128]{5,4,3,2,1,0:T(8,128)S(1)} %get-tuple-element.264), custom_call_target="InvertDiagBlocksLowerTriangular" | custom-call | tf_op jit(solution)/shard_map/jit(cholesky)/cholesky | solution.py:138
  372.1 1.9 fusion.17
  374.0 46.9 %custom-call.30 = f32[1,4,2,64,64]{4,3,2,1,0:T(8,128)S(1)} custom-call(f32[1,4,2,64,64]{4,3,2,1,0:T(8,128)S(1)} %fusion.17), custom_call_target="Cholesky" | custom-call | tf_op jit(solution)/shard_map/jit(cholesky)/cholesky | solution.py:138
  422.5 2.7 bitcast_select_fusion
  425.3 1.8 copy-done.3
  427.1 8.4 while.19
  427.7 3.6 bitcast_dynamic-update-slice_fusion.2
  431.9 3.5 bitcast_dynamic-update-slice_fusion.2
  437.0 236.9 %custom-call.31 = f32[4,2,3,128,128]{3,4,2,1,0:T(8,128)} custom-call(f32[4,2,3,128,128]{4,3,2,1,0:T(8,128)S(1)} %pad_maximum_fusion), custom_call_target="InvertDiagBlocksLowerTriangular" | custom-call | tf_op jit(solution)/shard_map/jit(_solve_triangular)/vmap(vmap())/triangular_solve | solution.py:139
  674.0 2.3 fusion.43
  676.3 2.3 convolution_subtract_fusion
  678.6 2.2 fusion.56
  681.0 3.4 fusion.12
  684.4 3.3 fusion.70
  688.3 10.2 fusion
  698.5 81.4 %psum.70 = f32[]{:T(128)} all-reduce(f32[]{:T(128)} %multiply_reduce_fusion.2), channel_id=1, replica_groups=mesh['gx'=4,'gy'=16,'gz'=4] {'gx','gy','gz'}, use_global_device_ids=true, to_apply=%region_7.8 | all-reduce | flops 1 | bytes 8 | tf_op jit(solution)/shard_map/psum | solution.py:150
  780.5 5.7 fusion.108
  786.2 1.9 collective-permute-start
  792.3 2.8 collective-permute-start.5
  813.4 4.9 fusion.106
  857.6 2.7 collective-permute-start.3
  860.4 1.9 collective-permute-start.4
  867.2 4.9 collective-permute-start.6
  896.6 1.7 fusion.148
  900.0 1.8 pad_add_fusion.7
  911.7 11.3 psum.71
  922.9 123.9 %psum.72 = f32[]{:T(128)} all-reduce(f32[]{:T(128)} %bitcast.81), channel_id=1, replica_groups=mesh['gx'=4,'gy'=16,'gz'=4] {'gy','gz'}, use_global_device_ids=true, to_apply=%region_10.11 | all-reduce | flops 1 | bytes 8 | tf_op jit(solution)/shard_map/psum | solution.py:162
  1048.1 76.9 %psum.73 = f32[]{:T(128)} all-reduce(f32[]{:T(128)} %multiply_reduce_fusion.1), channel_id=1, replica_groups=mesh['gx'=4,'gy'=16,'gz'=4] {'gx','gy','gz'}, use_global_device_ids=true, to_apply=%region_12.13 | all-reduce | flops 1 | bytes 8 | tf_op jit(solution)/shard_map/psum | solution.py:165
  1126.4 5.7 fusion.104
  1132.7 3.8 collective-permute-start.9
  1136.5 1.7 collective-permute-start.10
  1141.1 4.9 fusion.102
  1176.7 4.3 collective-permute-start.11
  1181.1 1.9 collective-permute-start.12
  1184.8 1.9 add.383
  1188.1 1.9 collective-permute-start.13
  1203.4 1.7 fusion.146
  1212.8 1.8 pad_add_fusion.4
  1227.4 9.5 psum.74
  1236.9 123.1 %psum.75 = f32[2]{0:T(128)S(1)} all-reduce(f32[2]{0:T(128)S(1)} %psum.74), channel_id=1, replica_groups=mesh['gx'=4,'gy'=16,'gz'=4] {'gy','gz'}, use_global_device_ids=true, to_apply=%region_16.17 | all-reduce | flops 2 | bytes 16 | tf_op jit(solution)/shard_map/psum | solution.py:162
  1360.7 1.8 multiply_reduce_fusion
  1362.5 77.3 %psum.76 = f32[]{:T(128)} all-reduce(f32[]{:T(128)} %get-tuple-element.257), channel_id=1, replica_groups=mesh['gx'=4,'gy'=16,'gz'=4] {'gx','gy','gz'}, use_global_device_ids=true, to_apply=%region_18.19 | all-reduce | flops 1 | bytes 8 | tf_op jit(solution)/shard_map/psum | solution.py:165
  1440.5 5.7 fusion.100
  1446.8 3.8 collective-permute-start.15
  1455.1 4.9 fusion.98
  1467.5 1.6 reshape_squeeze.177
  1489.8 4.3 collective-permute-start.17
  1494.2 1.9 collective-permute-start.18
  1518.5 2.0 pad_maximum_fusion.38
  1520.5 9.5 psum.77
  1530.0 122.5 %psum.78 = f32[3]{0:T(128)S(1)} all-reduce(f32[3]{0:T(128)S(1)} %psum.77), channel_id=1, replica_groups=mesh['gx'=4,'gy'=16,'gz'=4] {'gy','gz'}, use_global_device_ids=true, to_apply=%region_23.24 | all-reduce | flops 3 | bytes 24 | tf_op jit(solution)/shard_map/psum | solution.py:162
  1656.9 2.5 fusion.110
  1659.4 77.2 %psum.79 = f32[]{:T(128)} all-reduce(f32[]{:T(128)} %fusion.110), channel_id=1, replica_groups=mesh['gx'=4,'gy'=16,'gz'=4] {'gx','gy','gz'}, use_global_device_ids=true, to_apply=%region_25.26 | all-reduce | flops 1 | bytes 8 | tf_op jit(solution)/shard_map/psum | solution.py:165
  1737.6 5.7 fusion.96
  (389 shorter events, 237.8 us)
Async XLA Ops:
  0.0 1.8 copy-start
  0.0 5.9 copy-start.5
  15.1 1.9 copy-start.4
  425.2 1.9 copy-start.3
  427.1 247.0 %copy-start.8 = (f32[128,320]{0,1:T(8,128)S(1)}, f32[128,320]{0,1:T(8,128)}, u32[]{:S(2)}) copy-start(f32[128,320]{0,1:T(8,128)} %get-tuple-element.267) | copy-start | bytes 491524
  435.4 240.8 %copy-start.7 = (f32[128,320]{0,1:T(8,128)S(1)}, f32[128,320]{0,1:T(8,128)}, u32[]{:S(2)}) copy-start(f32[128,320]{0,1:T(8,128)} %get-tuple-element.266) | copy-start | bytes 491524
  674.0 6.8 slice-start
  680.8 6.8 copy-start.6
  698.4 91.0 %copy-start.2 = (f32[1,4,2,3,80,160]{5,4,3,2,1,0:T(8,128)S(1)}, f32[1,4,2,3,80,160]{5,4,3,2,1,0:T(8,128)}, u32[]{:S(2)}) copy-start(f32[1,4,2,3,80,160]{5,4,3,2,1,0:T(8,128)} %param.43) | copy-start | bytes 3686404
  698.5 98.8 %copy-start.12 = (s32[1,4,2,6]{3,2,1,0:T(2,128)S(1)}, s32[1,4,2,6]{3,2,1,0:T(2,128)}, u32[]{:S(2)}) copy-start(s32[1,4,2,6]{3,2,1,0:T(2,128)} %param.44) | copy-start | bytes 580
  786.2 61.6 %collective-permute-start = (f32[1,4,2,320]{3,1,2,0:T(4,128)S(1)}, f32[1,4,2,320]{3,1,2,0:T(4,128)}, u32[]{:S(2)}, u32[]{:S(2)}) collective-permute-start(f32[1,4,2,320]{3,1,2,0:T(4,128)S(1)} %bitcast.399), channel_id=1, source_target_pairs={{0,64},{64,128},{128,192},{1,65},{65,129},{129,193},{2,66},{66,130... | collective-permute-start | bytes 30728 | tf_op jit(solution)/shard_map/ppermute | solution.py:29
  788.1 65.2 %collective-permute-start.1 = (f32[1,4,2,320]{3,1,2,0:T(4,128)S(1)}, f32[1,4,2,320]{3,1,2,0:T(4,128)}, u32[]{:S(2)}, u32[]{:S(2)}) collective-permute-start(f32[1,4,2,320]{3,1,2,0:T(4,128)S(1)} %bitcast.400), channel_id=1, source_target_pairs={{64,0},{128,64},{192,128},{65,1},{129,65},{193,129},{66,2},{130,66... | collective-permute-start | bytes 30728 | tf_op jit(solution)/shard_map/ppermute | solution.py:31
  790.3 117.2 %collective-permute-start.2 = (f32[1,4,2,80,160]{4,3,2,1,0:T(8,128)}, f32[1,4,2,80,160]{4,3,2,1,0:T(8,128)S(1)}, u32[]{:S(2)}, u32[]{:S(2)}) collective-permute-start(f32[1,4,2,80,160]{4,3,2,1,0:T(8,128)} %slice_bitcast_fusion.2), channel_id=1, source_target_pairs={{64,0},{128,64},{192,128},{65,1},{129,65},{193,129},{66,2},{130,66... | collective-permute-start | bytes 1228808 | tf_op jit(solution)/shard_map/ppermute | solution.py:18
  792.3 103.3 %collective-permute-start.5 = (f32[1,1,2,80,160]{4,3,2,1,0:T(8,128)}, f32[1,1,2,80,160]{4,3,2,1,0:T(8,128)S(1)}, u32[]{:S(2)}, u32[]{:S(2)}) collective-permute-start(f32[1,1,2,80,160]{4,3,2,1,0:T(8,128)} %slice_bitcast_fusion.16), channel_id=1, source_target_pairs={{4,0},{8,4},{12,8},{16,12},{20,16},{24,20},{28,24},{32,28},{36,32}... | collective-permute-start | bytes 307208 | tf_op jit(solution)/shard_map/ppermute | solution.py:18
  795.9 107.2 %collective-permute-start.8 = (f32[1,4,1,80,160]{4,3,1,2,0:T(8,128)}, f32[1,4,1,80,160]{4,3,1,2,0:T(8,128)S(1)}, u32[]{:S(2)}, u32[]{:S(2)}) collective-permute-start(f32[1,4,1,80,160]{4,3,1,2,0:T(8,128)} %slice_bitcast_fusion.11), channel_id=1, source_target_pairs={{1,0},{2,1},{3,2},{5,4},{6,5},{7,6},{9,8},{10,9},{11,10},{13,12},{... | collective-permute-start | bytes 614408 | tf_op jit(solution)/shard_map/ppermute | solution.py:18
  842.9 53.6 %copy-start.20 = (f32[4,2]{1,0:T(4,128)}, f32[4,2]{1,0:T(4,128)S(1)}, u32[]{:S(2)}) copy-start(f32[4,2]{1,0:T(4,128)S(1)} %copy.392) | copy-start | bytes 100
  843.7 52.8 %copy-start.21 = (f32[4,2]{1,0:T(4,128)}, f32[4,2]{1,0:T(4,128)S(1)}, u32[]{:S(2)}) copy-start(f32[4,2]{1,0:T(4,128)S(1)} %copy.394) | copy-start | bytes 100
  857.6 7.6 collective-permute-start.3
  860.4 5.4 collective-permute-start.4
  865.2 0.6 copy-start.17
  867.2 11.3 collective-permute-start.6
  875.7 16.5 collective-permute-start.7
  883.8 12.7 copy-start.24
  898.4 11.4 copy-start.9
  1132.7 29.3 %collective-permute-start.9 = (f32[1,4,2,320]{3,1,2,0:T(4,128)}, f32[1,4,2,320]{3,1,2,0:T(4,128)}, u32[]{:S(2)}, u32[]{:S(2)}) collective-permute-start(f32[1,4,2,320]{3,1,2,0:T(4,128)} %bitcast.314.clone.2), channel_id=1, source_target_pairs={{0,64},{64,128},{128,192},{1,65},{65,129},{129,193},{2,66},{66,130... | collective-permute-start | bytes 30728 | tf_op jit(solution)/shard_map/ppermute | solution.py:29
  1136.5 31.8 %collective-permute-start.10 = (f32[1,4,2,320]{3,1,2,0:T(4,128)}, f32[1,4,2,320]{3,1,2,0:T(4,128)}, u32[]{:S(2)}, u32[]{:S(2)}) collective-permute-start(f32[1,4,2,320]{3,1,2,0:T(4,128)} %bitcast.314.clone.2), channel_id=1, source_target_pairs={{64,0},{128,64},{192,128},{65,1},{129,65},{193,129},{66,2},{130,66... | collective-permute-start | bytes 30728 | tf_op jit(solution)/shard_map/ppermute | solution.py:31
  1141.1 32.0 %copy-start.22 = (f32[4,2]{1,0:T(4,128)S(1)}, f32[4,2]{1,0:T(4,128)}, u32[]{:S(2)}) copy-start(f32[4,2]{1,0:T(4,128)} %copy.377) | copy-start | bytes 100
  1141.1 32.0 %copy-start.23 = (f32[4,2]{1,0:T(4,128)S(1)}, f32[4,2]{1,0:T(4,128)}, u32[]{:S(2)}) copy-start(f32[4,2]{1,0:T(4,128)} %copy.379) | copy-start | bytes 100
  1176.7 9.9 collective-permute-start.11
  1181.1 41.5 %copy-start.18 = (f32[4,2]{1,0:T(4,128)S(1)}, f32[4,2]{1,0:T(4,128)}, u32[]{:S(2)}) copy-start(f32[4,2]{1,0:T(4,128)} %copy.397) | copy-start | bytes 100
  1181.1 41.5 %copy-start.19 = (f32[4,2]{1,0:T(4,128)S(1)}, f32[4,2]{1,0:T(4,128)}, u32[]{:S(2)}) copy-start(f32[4,2]{1,0:T(4,128)} %copy.401) | copy-start | bytes 100
  1181.1 5.5 collective-permute-start.12
  1188.1 8.6 collective-permute-start.13
  1195.3 23.4 %collective-permute-start.14 = (f32[3,6,1,320]{3,1,2,0:T(8,128)}, f32[3,6,1,320]{3,1,2,0:T(8,128)}, u32[]{:S(2)}, u32[]{:S(2)}) collective-permute-start(f32[3,6,1,320]{3,1,2,0:T(8,128)} %get-tuple-element.285), channel_id=1, source_target_pairs={{1,0},{2,1},{3,2},{5,4},{6,5},{7,6},{9,8},{10,9},{11,10},{13,12},{... | collective-permute-start | bytes 69128 | tf_op jit(solution)/shard_map/ppermute | solution.py:31
  1202.6 0.8 copy-start.25
  1211.4 14.0 copy-start.14
  1211.4 14.0 copy-start.16
  1362.5 90.4 %copy-start.10 = (f32[1,4,2,320]{3,2,1,0:T(2,128)}, f32[1,4,2,320]{3,2,1,0:T(2,128)S(1)}, u32[]{:S(2)}) copy-start(f32[1,4,2,320]{3,2,1,0:T(2,128)S(1)} %get-tuple-element.258) | copy-start | bytes 30724
  1446.8 29.5 %collective-permute-start.15 = (f32[1,4,2,320]{3,1,2,0:T(4,128)}, f32[1,4,2,320]{3,1,2,0:T(4,128)}, u32[]{:S(2)}, u32[]{:S(2)}) collective-permute-start(f32[1,4,2,320]{3,1,2,0:T(4,128)} %bitcast.311.clone.2), channel_id=1, source_target_pairs={{0,64},{64,128},{128,192},{1,65},{65,129},{129,193},{2,66},{66,130... | collective-permute-start | bytes 30728 | tf_op jit(solution)/shard_map/ppermute | solution.py:29
  1450.7 32.0 %collective-permute-start.16 = (f32[1,4,2,320]{3,1,2,0:T(4,128)}, f32[1,4,2,320]{3,1,2,0:T(4,128)}, u32[]{:S(2)}, u32[]{:S(2)}) collective-permute-start(f32[1,4,2,320]{3,1,2,0:T(4,128)} %bitcast.311.clone.2), channel_id=1, source_target_pairs={{64,0},{128,64},{192,128},{65,1},{129,65},{193,129},{66,2},{130,66... | collective-permute-start | bytes 30728 | tf_op jit(solution)/shard_map/ppermute | solution.py:31
  1489.8 8.2 collective-permute-start.17
  1494.2 5.3 collective-permute-start.18
  1500.3 4.9 collective-permute-start.19
  1503.6 10.9 collective-permute-start.20
  1506.4 11.4 copy-start.11
  1506.4 11.4 copy-start.13
  1506.4 11.4 copy-start.15
  1513.7 230.2 %copy-start.1 = (bf16[1,4,2,320,320]{4,3,2,1,0:T(8,128)(2,1)S(1)}, bf16[1,4,2,320,320]{4,3,2,1,0:T(8,128)(2,1)}, u32[]{:S(2)}) copy-start(bf16[1,4,2,320,320]{4,3,2,1,0:T(8,128)(2,1)} %param.41) | copy-start | bytes 4915204
